TPU v7x, 128 devices: a whole 4x4x4 slice. The times are simulated.
128 devices in a mesh: rep: 16 (over x_lo, y, core), fsdp: 8 (over x_hi, z).
Axes of the slice: x: 4 (x_hi: 2, x_lo: 2; x = x_hi * 2 + x_lo), y: 4, z: 4, core: 2. Of those that a mesh axis runs over, the one named last changes fastest.
Arguments:
- tokens: bfloat16 [131072, 8192], P(('rep', 'fsdp')), may hold values from -6 to 6
- norm_gain: bfloat16 [8192], replicated, may hold values from 0.25 to 1.75
- deltas: bfloat16 [16, 8192, 1024], P('rep', 'fsdp'), may hold values from -0.09375 to 0.09375
- inner_steps: int32 [16, 16], replicated, may hold values from 1 to 64
- bucket_of_row: int32 [8192], P('fsdp'), may hold values from 0 to 15, never falling along the last dimension, each value on 1 to 1024 neighbouring positions
- master: float32 [8192, 1024], P(('fsdp', 'rep')), may hold values from -0.0625 to 0.0625
- momentum: float32 [8192, 1024], P(('fsdp', 'rep')), may hold values from -0.0625 to 0.0625
Outputs:
- keys: bfloat16 [131072, 1024], P(('rep', 'fsdp'))
- master_new: float32 [8192, 1024], P(('fsdp', 'rep'))
- momentum_new: float32 [8192, 1024], P(('fsdp', 'rep'))
Inputs may be any that keep to these rules, and one draw needn't show every extreme that they name: `bucket_of_row`: never falls along the rows; each bucket holds 1 to 1024 rows.
All inputs are finite; a program needn't handle non-finite values.
Results may differ from a plain program's by a relative error of at most 0.0058.
Values may be sent and summed in bfloat16 or wider, within the bound.
A program may use at most 192 MiB of HBM per device.

v0:
```python
import jax
import jax.numpy as jnp
from jax import lax
from jax.sharding import PartitionSpec as P

OUTER_RATE = 0.7
MOMENTUM_KEEP = 0.9
EPSILON = 1e-05


def normalize(rows, norm_gain):
    values = rows.astype(jnp.float32)
    scale = lax.rsqrt(jnp.mean(values * values, axis=1, keepdims=True) + EPSILON)
    return (values * scale * norm_gain.astype(jnp.float32)[None, :]).astype(jnp.bfloat16)


def on_device(tokens, norm_gain, deltas, inner_steps, bucket_of_row, master, momentum):
    counts = inner_steps.astype(jnp.float32)
    share = counts / jnp.sum(counts, axis=0, keepdims=True)
    own_share = lax.dynamic_slice_in_dim(share, lax.axis_index("rep"), 1, 0)[0]
    bucket_ids = jnp.arange(counts.shape[1], dtype=jnp.int32)
    one_hot = (bucket_of_row[:, None] == bucket_ids[None, :]).astype(jnp.float32)
    row_weight = jnp.sum(one_hot * own_share[None, :], axis=1)
    weighted = row_weight[:, None] * deltas[0].astype(jnp.float32)
    averaged = lax.psum_scatter(weighted, "rep", scatter_dimension=0, tiled=True)
    momentum_new = MOMENTUM_KEEP * momentum + averaged
    master_new = master - OUTER_RATE * (averaged + MOMENTUM_KEEP * momentum_new)
    layer = master_new.astype(jnp.bfloat16)
    normed = normalize(tokens, norm_gain)
    fsdp_count = lax.axis_size("fsdp")
    rep_count = lax.axis_size("rep")
    shard_len = layer.shape[0]
    piece = lax.all_gather(layer, ("rep", "fsdp"), axis=0, tiled=True)
    order = jnp.arange(piece.shape[0], dtype=jnp.int32)
    shard = order // shard_len
    within = order % shard_len
    rep_pos = shard // fsdp_count
    fsdp_pos = shard % fsdp_count
    column_ids = (fsdp_pos * rep_count + rep_pos) * shard_len + within
    columns = jnp.take(normed, column_ids, axis=1)
    projected = jnp.dot(columns, piece, preferred_element_type=jnp.float32)
    return (projected.astype(jnp.bfloat16), master_new, momentum_new)


def solution(mesh):
    in_specs = (
        P(("rep", "fsdp"), None),
        P(),
        P("rep", "fsdp", None),
        P(),
        P("fsdp"),
        P(("fsdp", "rep"), None),
        P(("fsdp", "rep"), None),
    )
    out_specs = (P(("rep", "fsdp"), None), P(("fsdp", "rep"), None), P(("fsdp", "rep"), None))
    return jax.shard_map(
        on_device, mesh=mesh, in_specs=in_specs, out_specs=out_specs, check_vma=False
    )
```

profile of v0, /device:TPU:1, one launch (start us, length us, event | category | flops | bytes accessed | tf_op | source)
XLA Modules:
  0.0 442.1 jit_solution(9010786290908330354)
XLA Ops:
  7.2 0.0 reduce-scatter.2.cloned.1.call-start
  7.2 0.7 convert_element_type.28
  7.9 0.7 convert_reduce_fusion
  8.6 0.8 select_reduce_fusion
  9.4 3.9 convert_multiply_fusion.2
  13.3 0.0 reduce-scatter.2.cloned.1.call-update
  13.3 0.0 all-gather.2.cloned.1.call-start
  13.3 66.3 %reduce-scatter.2.cloned.1.call-done = f32[64,1024]{1,0:T(8,128)} async-done(((f32[1024,1024]{1,0:T(8,128)}), f32[64,1024]{1,0:T(8,128)}) %reduce-scatter.2.cloned.1.call-update) | async-done | bytes 262160 | tf_op jit(solution)/shard_map/reduce_scatter | solution.py:25
  79.7 2.0 fusion.33
  81.7 0.0 all-gather.2.cloned.1.call-update
  81.7 0.0 copy-start.1
  81.7 22.4 %copy.12 = bf16[1024,8192]{0,1:T(8,128)(2,1)} copy(bf16[1024,8192]{1,0:T(8,128)(2,1)} %param.7) | data formatting | bytes 33554432 | tf_op args[0]
  104.2 0.0 copy-done.1
  104.2 0.0 copy-start
  104.2 10.5 %fusion = f32[1024]{0:T(1024)S(1)} fusion(bf16[1024,8192]{0,1:T(8,128)(2,1)} %copy.12), kind=kLoop, calls=%fused_computation.3 | loop fusion | flops 25164800 | bytes 16781312 | tf_op jit(solution)/shard_map/reduce_sum | solution.py:13
  114.7 0.1 compare_select_fusion
  114.8 0.5 copy-done
  115.3 8.0 %fusion.2 = bf16[1024,8192]{0,1:T(8,128)(2,1)} fusion(bf16[1024,8192]{0,1:T(8,128)(2,1)S(1)} %copy-done, f32[8192]{0:T(1024)S(1)} %convert_element_type.26, f32[1024]{0:T(1024)S(1)} %add_rsqrt_fusion), kind=kLoop, calls=%fused_computation.5 | loop fusion | flops 33554432 | bytes 33591296 | tf_op jit(solution)/shard_map/convert_element_type | solution.py:14
  123.3 48.7 %gather_fusion = bf16[8192,1024]{1,0:T(8,128)(2,1)} fusion(bf16[1024,8192]{0,1:T(8,128)(2,1)} %fusion.2, s32[8192]{0:T(1024)S(1)} %broadcast_clamp_fusion), kind=kCustom, calls=%fused_computation | custom fusion | bytes 33587200 | tf_op jit(solution)/shard_map/jit(_take)/gather | solution.py:40
  172.0 239.4 %all-gather.2.cloned.1.call-done = bf16[8192,1024]{1,0:T(8,128)(2,1)} async-done(((bf16[64,1024]{1,0:T(8,128)(2,1)}), bf16[8192,1024]{1,0:T(8,128)(2,1)}) %all-gather.2.cloned.1.call-update) | async-done | bytes 16777232 | tf_op jit(solution)/shard_map/all_gather | solution.py:33
  411.4 23.8 %fusion.7 = bf16[1024,1024]{1,0:T(8,128)(2,1)} fusion(bf16[8192,1024]{1,0:T(8,128)(2,1)} %all-gather.2.cloned.1.call-done, bf16[8192,1024]{1,0:T(8,128)(2,1)} %gather_fusion, pred[8192]{0:T(1024)(128)(4,1)S(1)} %compare_and_fusion), kind=kOutput, calls=%fused_computation.11 | convolution fusion | flops 17189306368 | bytes 35659776 | tf_op jit(solution)/shard_map/dot_general | solution.py:41
  (5 shorter events, 0.1 us)
Async XLA Ops:
  7.2 72.5 %reduce-scatter.2.cloned.1.call-start = ((), (), s32[]{:S(2)}) async-start(), calls=%async_computation.1 | async-start | bytes 4456448 | tf_op jit(solution)/shard_map/reduce_scatter | solution.py:25
  13.3 398.1 %all-gather.2.cloned.1.call-start = ((), (), s32[]{:S(2)}) async-start(), calls=%async_computation.2 | async-start | bytes 16908288 | tf_op jit(solution)/shard_map/all_gather | solution.py:33
  81.7 22.4 %copy-start.1 = (bf16[8192]{0:T(1024)(128)(2,1)S(1)}, bf16[8192]{0:T(1024)(128)(2,1)}, u32[]{:S(2)}) copy-start(bf16[8192]{0:T(1024)(128)(2,1)} %param.8) | copy-start | bytes 49156
  104.2 11.1 %copy-start = (bf16[1024,8192]{0,1:T(8,128)(2,1)S(1)}, bf16[1024,8192]{0,1:T(8,128)(2,1)}, u32[]{:S(2)}) copy-start(bf16[1024,8192]{0,1:T(8,128)(2,1)} %copy.12) | copy-start | bytes 50331652
Sparse Core Ops, SparseCore 0:
  13.4 66.2 reduce-scatter.1
  81.9 329.4 all-gather.1
where the time goes:
time: 443 us; the launch traced here: 442 us
  waiting for transfers between devices  306 us (69%)
  local copies, waits for them, and re-layouts  71.6 us (16%)
  other arithmetic  26.7 us (6%)
  matrix products  23.8 us (5%)
  between operations  14.1 us (3%)
    all_gather x1, waiting for transfers between devices, on_device(): piece = lax.all_gather(layer, ('rep', 'fsdp'), axis=0, tiled=True)  239 us
    reduce_scatter x1, waiting for transfers between devices, on_device(): lax.psum_scatter(weighted, 'rep', scatter_dimension=0, tiled=True)  66.3 us
    gather x1, local copies, waits for them, and re-layouts, on_device(): columns = jnp.take(normed, column_ids, axis=1)  48.7 us
    dot_general x1, matrix products, on_device(): projected = jnp.dot(columns, piece, preferred_element_type=jnp.float32)  23.8 us
    unnamed x5, local copies, waits for them, and re-layouts  22.9 us
    reduce_sum x1, other arithmetic, normalize(): jnp.mean(values * values, axis=1, keepdims=True) + EPSILON  10.5 us
  transfers between devices with their start and end apart: 2, of which 2 were waited for; matrix products, arithmetic and copies ran while one was open for 20% of the time, Pallas kernels for 0%

commit v1 on v0

v1 whole, which is shorter than its diff:
```python
import jax
import jax.numpy as jnp
from jax import lax
from jax.experimental import pallas as pl
from jax.experimental.pallas import tpu as pltpu
from jax.sharding import PartitionSpec as P

OUTER_RATE = 0.7
MOMENTUM_KEEP = 0.9
EPSILON = 1e-05
MESH = pl.DeviceIdType.MESH
F32 = jnp.float32
BF16 = jnp.bfloat16

PARTS = 4
COLS = 256
ROWS = 64
TILE = 256
LINE, PLANE, CUBE, FORWARD, SIBLING, COPIES = 0, 3, 6, 14, 18, 34


def mod4(v):
    return lax.rem(v + 8, 4)


def position():
    rep = lax.axis_index("rep")
    fsdp = lax.axis_index("fsdp")
    x = lax.div(fsdp, 4) * 2 + lax.div(rep, 8)
    y = lax.rem(lax.div(rep, 2), 4)
    z = lax.rem(fsdp, 4)
    return x, y, z, lax.rem(rep, 2)


def device(x, y, z, core):
    return (lax.rem(x, 2) * 8 + y * 2 + core, lax.div(x, 2) * 4 + z)


def choose(axis, x, y, z):
    return lax.div(2 - axis, 2) * x + lax.rem(axis, 2) * y + lax.div(axis, 2) * z


def roles(part):
    return lax.rem(part, 3), lax.rem(part + 1, 3), lax.rem(part + 2, 3)


def kernel(tokens, gain, deltas, steps, bucket, master, momentum,
           keys, master_out, momentum_out,
           tok, layer, acc, own, sib, pairs, landed, mas, mom, gain_v, steps_v, bucket_v,
           wcol, inv, out, local, pair_sem, red_s, red_r, gat_s, gat_r):
    x, y, z, core = position()
    chip = lax.rem(x, 2) * 4 + y
    sibling = device(x, y, z, 1 - core)

    def local_copy(src, dst, i):
        return pltpu.make_async_copy(src, dst, local.at[i])

    own_copy = local_copy(deltas.at[:, core], own, 0)
    steps_copy = local_copy(steps, steps_v, 1)
    bucket_copy = local_copy(bucket, bucket_v, 2)
    gain_copy = local_copy(gain, gain_v, 3)
    mas_copy = local_copy(master, mas, 4)
    mom_copy = local_copy(momentum, mom, 5)
    for copy in (steps_copy, bucket_copy, own_copy, gain_copy, mas_copy, mom_copy):
        copy.start()

    barrier = pltpu.get_barrier_semaphore()
    peers = [sibling]
    for d in range(1, 8):
        k = lax.rem(chip + d, 8)
        peers.append(device(lax.div(x, 2) * 2 + lax.div(k, 4), lax.rem(k, 4), z, core))
    far = (1 - lax.div(x, 2)) * 2
    peers.append(device(far, y, z, core))
    peers.append(device(far + 1, y, z, core))
    for d in range(1, 4):
        peers.append(device(x, y, mod4(z + d), core))
    for peer in peers:
        pl.semaphore_signal(barrier, inc=1, device_id=peer, device_id_type=MESH)
    pl.semaphore_wait(barrier, len(peers))

    pair_copy = pltpu.make_async_remote_copy(
        src_ref=deltas.at[:, 1 - core], dst_ref=sib, send_sem=pair_sem.at[0], recv_sem=pair_sem.at[1],
        device_id=sibling, device_id_type=MESH)
    pair_copy.start()
    tok_copies = [local_copy(tokens.at[pl.ds(i * TILE, TILE)], tok.at[pl.ds(i * TILE, TILE)], 6 + i) for i in range(4)]
    for copy in tok_copies:
        copy.start()

    steps_copy.wait()
    bucket_copy.wait()
    counts = steps_v[...].astype(F32)
    share = counts / jnp.sum(counts, axis=0, keepdims=True)
    replica = lax.axis_index("rep")
    replica_ids = lax.broadcasted_iota(jnp.int32, (16, 16), 0)
    lane = lax.broadcasted_iota(jnp.int32, (ROWS, 128), 1)
    row = lax.broadcasted_iota(jnp.int32, (ROWS, 128), 0)
    mine = lane == row + core * ROWS
    buckets = bucket_v[...]
    for side, who in enumerate((replica, replica + 1 - 2 * core)):
        row_share = jnp.sum(jnp.where(replica_ids == who, share, 0.0), axis=0, keepdims=True)
        weight = jnp.zeros((8, 128), F32)
        for b in range(16):
            weight = weight + jnp.where(buckets == b, row_share[:, b:b + 1], 0.0)
        for k in range(8):
            column = jnp.sum(jnp.where(mine, weight[k:k + 1, :], 0.0), axis=1, keepdims=True)
            wcol[side, k] = jnp.broadcast_to(column, (ROWS, 128))

    own_copy.wait()
    pair_copy.wait()

    def reduce_copy(part, d):
        k = lax.rem(chip + d, 8)
        return pltpu.make_async_remote_copy(
            src_ref=pairs.at[part, k], dst_ref=landed.at[part, d - 1],
            send_sem=red_s.at[part, d - 1], recv_sem=red_r.at[part, d - 1],
            device_id=device(lax.div(x, 2) * 2 + lax.div(k, 4), lax.rem(k, 4), z, core), device_id_type=MESH)

    @pl.loop(0, PARTS)
    def _(part):
        columns = pl.ds(pl.multiple_of(part * COLS, COLS), COLS)

        @pl.loop(0, 8)
        def _(k):
            w0 = wcol[0, k][:, :1]
            w1 = wcol[1, k][:, :1]
            both = w0 * own[k, :, columns].astype(F32) + w1 * sib[k, :, columns].astype(F32)
            pairs[part, k] = both.astype(BF16)

        @pl.loop(1, 8)
        def _(d):
            reduce_copy(part, d).start()

    acc[...] = jnp.zeros_like(acc)
    gain_copy.wait()
    gain_row = gain_v[pl.ds(lax.axis_index("fsdp") * 8 + chip, 1), :]
    gain_col = jnp.sum(jnp.where(mine, gain_row, 0.0), axis=1, keepdims=True)
    mas_copy.wait()
    mom_copy.wait()
    for copy in tok_copies:
        copy.wait()

    @pl.loop(0, 1024 // 32)
    def _(i):
        rows = pl.ds(pl.multiple_of(i * 32, 32), 32)
        total = jnp.zeros((32, 128), F32)
        for j in range(64):
            v = tok[rows, j * 128:(j + 1) * 128].astype(F32)
            total = total + v * v
        mean = jnp.sum(total, axis=1, keepdims=True) * (1.0 / 8192.0)
        inv[rows, :] = jnp.broadcast_to(lax.rsqrt(mean + EPSILON), (32, 128))

    def place(part):
        q1, q2, q3 = roles(part)
        return choose(q1, x, y, z), choose(q2, x, y, z), choose(q3, x, y, z)

    def along(axis, d):
        return device(mod4(x + lax.div(2 - axis, 2) * d), mod4(y + lax.rem(axis, 2) * d), mod4(z + lax.div(axis, 2) * d), core)

    def gather_copy(part, ref, index, target):
        return pltpu.make_async_remote_copy(
            src_ref=ref, dst_ref=ref, send_sem=gat_s.at[part, index], recv_sem=gat_r.at[part, index],
            device_id=target, device_id_type=MESH)

    def line_send(part, d):
        i1, i2, i3 = place(part)
        return gather_copy(part, layer.at[part, i3, i2, i1, core], LINE + d - 1, along(roles(part)[0], d))

    def line_recv(part, d):
        i1, i2, i3 = place(part)
        return gather_copy(part, layer.at[part, i3, i2, mod4(i1 - d), core], LINE + d - 1, sibling)

    def a_line(part, da3, da2, who):
        i1, i2, i3 = place(part)
        return layer.at[part, mod4(i3 + da3), mod4(i2 + da2), :, who]

    def plane_send(part, d):
        return gather_copy(part, a_line(part, 0, 0, core), PLANE + d - 1, along(roles(part)[1], d))

    def plane_recv(part, d):
        return gather_copy(part, a_line(part, 0, -d, core), PLANE + d - 1, sibling)

    def cube_send(part, way, j):
        return gather_copy(part, a_line(part, 0, -j, core), CUBE + way * 4 + j, along(roles(part)[2], 1 - 2 * way))

    def cube_recv(part, way, j):
        return gather_copy(part, a_line(part, 2 * way - 1, -j, core), CUBE + way * 4 + j, sibling)

    def forward_send(part, way, j):
        return gather_copy(part, a_line(part, 2 * way - 1, -j, core), FORWARD + j, along(roles(part)[2], 1 - 2 * way))

    def forward_recv(part, j):
        return gather_copy(part, a_line(part, 2, -j, core), FORWARD + j, sibling)

    SHIFT = (0, -1, 1, 2)

    def sibling_send(part, k, j):
        return gather_copy(part, a_line(part, SHIFT[k], -j, core), SIBLING + k * 4 + j, sibling)

    def sibling_recv(part, k, j):
        return gather_copy(part, a_line(part, SHIFT[k], -j, 1 - core), SIBLING + k * 4 + j, sibling)

    def multiply(part, k, j):
        q1, q2, q3 = roles(part)
        i1, i2, i3 = place(part)
        i3 = mod4(i3 + SHIFT[k])
        i2 = mod4(i2 - j)
        starts = []
        for i in range(4):
            cx, cy, cz = [
                (
                    same(q1, a) * i + same(q2, a) * i2 + same(q3, a) * i3) for a in range(3)]
            starts.append(pl.multiple_of(lax.div(cx, 2) * 4096 + cz * 1024 + lax.rem(cx, 2) * 512 + cy * 128, 128))
        weights = layer[part, i3, i2].reshape(8 * ROWS, COLS)

        @pl.loop(0, 1024 // TILE)
        def _(t):
            rows = pl.ds(pl.multiple_of(t * TILE, TILE), TILE)
            left = jnp.concatenate([tok[rows, pl.ds(s, 128)] for s in starts], axis=1)
            acc[part, rows, :] += jnp.dot(left, weights, preferred_element_type=F32)

    def same(q, a):
        if a == 0:
            return lax.div(2 - q, 2)
        return lax.rem(q, 2) if a == 1 else lax.div(q, 2)

    @pl.loop(0, PARTS)
    def _(part):
        columns = pl.ds(pl.multiple_of(part * COLS, COLS), COLS)

        @pl.loop(1, 8)
        def _(d):
            reduce_copy(part, d).wait_recv()

        averaged = pairs[part, chip].astype(F32)
        for d in range(7):
            averaged = averaged + landed[part, d].astype(F32)
        momentum_new = MOMENTUM_KEEP * mom[:, columns] + averaged
        master_new = mas[:, columns] - OUTER_RATE * (averaged + MOMENTUM_KEEP * momentum_new)
        mom[:, columns] = momentum_new
        mas[:, columns] = master_new
        i1, i2, i3 = place(part)
        layer[part, i3, i2, i1, core] = (gain_col * master_new).astype(BF16)
        for d in (1, 3, 2):
            line_send(part, d).start()

    mas_back = local_copy(mas, master_out, 4)
    mom_back = local_copy(mom, momentum_out, 5)
    mas_back.start()
    mom_back.start()

    @pl.loop(0, PARTS)
    def _(part):
        for d in (1, 3, 2):
            line_recv(part, d).wait_recv()
        for d in (1, 3, 2):
            plane_send(part, d).start()
        cube_send(part, 0, 0).start()
        cube_send(part, 1, 0).start()
        sibling_send(part, 0, 0).start()

    @pl.loop(1, 4)
    def _(d):
        @pl.loop(0, PARTS)
        def _(part):
            plane_recv(part, d).wait_recv()
            cube_send(part, 0, d).start()
            cube_send(part, 1, d).start()
            sibling_send(part, 0, d).start()
            sibling_recv(part, 0, d - 1).wait_recv()
            multiply(part, 0, d - 1)

    @pl.loop(0, 4)
    def _(j):
        @pl.loop(0, PARTS)
        def _(part):
            for way in (0, 1):
                cube_recv(part, way, j).wait_recv()
                sibling_send(part, 1 + way, j).start()

            @pl.when(lax.rem(j, 2) == 0)
            def _():
                forward_send(part, 0, j).start()

            @pl.when(lax.rem(j, 2) == 1)
            def _():
                forward_send(part, 1, j).start()

            @pl.when(j == 0)
            def _():
                sibling_recv(part, 0, 3).wait_recv()
                multiply(part, 0, 3)

            @pl.when(j > 0)
            def _():
                for k in (1, 2):
                    sibling_recv(part, k, j - 1).wait_recv()
                    multiply(part, k, j - 1)

    @pl.loop(0, 4)
    def _(j):
        @pl.loop(0, PARTS)
        def _(part):
            forward_recv(part, j).wait_recv()
            sibling_send(part, 3, j).start()

            @pl.when(j == 0)
            def _():
                for k in (1, 2):
                    sibling_recv(part, k, 3).wait_recv()
                    multiply(part, k, 3)

            @pl.when(j > 0)
            def _():
                sibling_recv(part, 3, j - 1).wait_recv()
                multiply(part, 3, j - 1)

    @pl.loop(0, PARTS)
    def _(part):
        sibling_recv(part, 3, 3).wait_recv()
        multiply(part, 3, 3)

    def keys_copy(t):
        rows = pl.ds(pl.multiple_of(t * TILE, TILE), TILE)
        return pltpu.make_async_copy(out.at[rows], keys.at[rows], local.at[6 + t])

    @pl.loop(0, 1024 // TILE)
    def _(t):
        rows = pl.ds(pl.multiple_of(t * TILE, TILE), TILE)
        scale = inv[rows, :][:, :1]
        for p in range(PARTS):
            out[rows, p * COLS:(p + 1) * COLS] = (acc[p, rows, :] * scale).astype(BF16)
        keys_copy(t).start()

    @pl.loop(0, PARTS)
    def _(part):
        @pl.loop(1, 8)
        def _(d):
            reduce_copy(part, d).wait_send()

        @pl.loop(1, 4)
        def _(d):
            line_send(part, d).wait_send()
            plane_send(part, d).wait_send()

        @pl.loop(0, 4)
        def _(j):
            cube_send(part, 0, j).wait_send()
            cube_send(part, 1, j).wait_send()
            forward_send(part, 0, j).wait_send()
            for k in range(4):
                sibling_send(part, k, j).wait_send()

    mas_back.wait()
    mom_back.wait()

    @pl.loop(0, 1024 // TILE)
    def _(t):
        keys_copy(t).wait()


def on_device(tokens, norm_gain, deltas, inner_steps, bucket_of_row, master, momentum):
    hbm = pl.BlockSpec(memory_space=pl.ANY)
    dma = pltpu.SemaphoreType.DMA
    return pl.pallas_call(
        kernel,
        out_shape=(
            jax.ShapeDtypeStruct((1024, 1024), BF16),
            jax.ShapeDtypeStruct((ROWS, 1024), F32),
            jax.ShapeDtypeStruct((ROWS, 1024), F32),
        ),
        in_specs=[hbm] * 7,
        out_specs=(hbm, hbm, hbm),
        scratch_shapes=[
            pltpu.VMEM((1024, 8192), BF16),
            pltpu.VMEM((PARTS, 4, 4, 4, 2, ROWS, COLS), BF16),
            pltpu.VMEM((PARTS, 1024, COLS), F32),
            pltpu.VMEM((8, ROWS, 1024), BF16),
            pltpu.VMEM((8, ROWS, 1024), BF16),
            pltpu.VMEM((PARTS, 8, ROWS, COLS), BF16),
            pltpu.VMEM((PARTS, 7, ROWS, COLS), BF16),
            pltpu.VMEM((ROWS, 1024), F32),
            pltpu.VMEM((ROWS, 1024), F32),
            pltpu.VMEM((64, 128), F32),
            pltpu.VMEM((16, 16), jnp.int32),
            pltpu.VMEM((8, 128), jnp.int32),
            pltpu.VMEM((2, 8, ROWS, 128), F32),
            pltpu.VMEM((1024, 128), F32),
            pltpu.VMEM((1024, 1024), BF16),
            dma((10,)),
            dma((2,)),
            dma((PARTS, 7)),
            dma((PARTS, 7)),
            dma((PARTS, COPIES)),
            dma((PARTS, COPIES)),
        ],
        compiler_params=pltpu.CompilerParams(
            collective_id=0, has_side_effects=True, vmem_limit_bytes=56 * 1024 * 1024),
        cost_estimate=pl.CostEstimate(flops=2 * 1024 * 8192 * 1024, bytes_accessed=24 << 20, transcendentals=1024),
    )(
        tokens,
        norm_gain.astype(F32).reshape(64, 128),
        deltas.reshape(8, 2, ROWS, 1024),
        inner_steps,
        bucket_of_row.reshape(8, 128),
        master,
        momentum,
    )


def solution(mesh):
    in_specs = (
        P(("rep", "fsdp"), None),
        P(),
        P("rep", "fsdp", None),
        P(),
        P("fsdp"),
        P(("fsdp", "rep"), None),
        P(("fsdp", "rep"), None),
    )
    out_specs = (P(("rep", "fsdp"), None), P(("fsdp", "rep"), None), P(("fsdp", "rep"), None))
    return jax.shard_map(
        on_device, mesh=mesh, in_specs=in_specs, out_specs=out_specs, check_vma=False
    )
```

time: 443 us -> 118 us (0.27)
  waiting for transfers between devices: 306 us -> 0 us
  Pallas kernels: 0 us -> 110 us
  local copies, waits for them, and re-layouts: 71.6 us -> 4.55 us
  other arithmetic: 26.7 us -> 1.34 us
  matrix products: 23.8 us -> 0 us
  between operations: 14.1 us -> 0.66 us
    all_gather x1 -> x0, waiting for transfers between devices: 239 us -> none  [on_device(): piece = lax.all_gather(layer, ('rep', 'fsdp'), axis=0, tiled=True)]
    pallas_call x0 -> x1, Pallas kernels: none -> 110 us  [on_device(): pl.pallas_call(kernel, out_shape=(jax.ShapeDtypeStruct((1024, 1024), BF16...]
    reduce_scatter x1 -> x0, waiting for transfers between devices: 66.3 us -> none  [on_device(): lax.psum_scatter(weighted, 'rep', scatter_dimension=0, tiled=True)]
    gather x1 -> x0, local copies, waits for them, and re-layouts: 48.7 us -> none  [on_device(): columns = jnp.take(normed, column_ids, axis=1)]
    dot_general x1 -> x0, matrix products: 23.8 us -> none  [on_device(): projected = jnp.dot(columns, piece, preferred_element_type=jnp.float32)]
    unnamed x5 -> x7, local copies, waits for them, and re-layouts: 22.9 us -> 4.55 us
    reduce_sum x3 -> x0, other arithmetic: 12 us -> none  [the longest x1 10.5 us: normalize(): jnp.mean(values * values, axis=1, keepdims=True) + EPSILON]
    convert_element_type x4 -> x0, other arithmetic: 10.7 us -> none  [the longest x1 8 us: normalize(): (values * scale * norm_gain.astype(jnp.float32)[None, :]).astype(jnp.bflo...]
  transfers between devices with their start and end apart: 2 -> 0, of which waited for: 2 -> 0; matrix products, arithmetic and copies ran while one was open for 20% -> 0% of each run, Pallas kernels for 0% -> 0%
where the time goes in v1:
time: 118 us; the launch traced here: 116 us
  Pallas kernels  110 us (93%)
  local copies, waits for them, and re-layouts  4.55 us (4%)
  other arithmetic  1.34 us (1%)
    pallas_call x1, Pallas kernels, on_device(): pl.pallas_call(kernel, out_shape=(jax.ShapeDtypeStruct((1024, 1024), BF16...  110 us
    unnamed x7, local copies, waits for them, and re-layouts  4.55 us

profile of v1, /device:TPU:1, one launch (start us, length us, event | category | flops | bytes accessed | tf_op | source)
XLA Modules:
  0.0 116.2 jit_solution(8335325123437895712)
XLA Ops:
  0.6 1.3 %bitcast_convert_fusion.gain = f32[64,128]{1,0:T(8,128)} fusion(bf16[8192]{0:T(1024)(128)(2,1)} %param.8), kind=kLoop, calls=%fused_computation | loop fusion | flops 8192 | bytes 49152 | tf_op jit(solution)/shard_map/reshape | solution.py:401
  2.0 109.7 %shard_map.94 = (bf16[1024,1024]{1,0:T(8,128)(2,1)}, f32[64,1024]{1,0:T(8,128)}, f32[64,1024]{1,0:T(8,128)}) custom-call(bf16[1024,8192]{1,0:T(8,128)(2,1)} %tokens.1, f32[64,128]{1,0:T(8,128)} %bitcast_convert_fusion.gain, bf16[8,2,64,1024]{3,2,1,0:T(8,128)(2,1)} %bitcast.5, s32[16,16]{1,0:T(8,128)} %steps.1, s32[8,128]{1,0:T(8,128)} %bitcast.6, ...), custom_call_target="tpu_custom_call" | custom-call | flops 17179869184 | bytes 25165824 | tf_op jit(solution)/shard_map/pallas_call | solution.py:364
  111.6 0.0 copy-start.1
  111.6 0.0 copy-start
  111.7 3.1 %copy.13 = bf16[1024,1024]{1,0:T(8,128)(2,1)} copy(bf16[1024,1024]{1,0:T(8,128)(2,1)} %get-tuple-element.6) | data formatting | bytes 4194304
  114.8 0.0 copy-done.1
  114.8 0.7 copy.14
  115.5 0.0 copy-done
  115.5 0.7 copy.15
Async XLA Ops:
  111.6 3.2 %copy-start.1 = (f32[64,1024]{1,0:T(8,128)S(1)}, f32[64,1024]{1,0:T(8,128)}, u32[]{:S(2)}) copy-start(f32[64,1024]{1,0:T(8,128)} %get-tuple-element.7) | copy-start | bytes 786436
  111.6 3.9 %copy-start = (f32[64,1024]{1,0:T(8,128)S(1)}, f32[64,1024]{1,0:T(8,128)}, u32[]{:S(2)}) copy-start(f32[64,1024]{1,0:T(8,128)} %get-tuple-element.8) | copy-start | bytes 786436

commit v2 on v1

v2 whole, which is shorter than its diff:
```python
import jax
import jax.numpy as jnp
from jax import lax
from jax.experimental import pallas as pl
from jax.experimental.pallas import tpu as pltpu
from jax.sharding import PartitionSpec as P

OUTER_RATE = 0.7
MOMENTUM_KEEP = 0.9
EPSILON = 1e-05
MESH = pl.DeviceIdType.MESH
F32 = jnp.float32
BF16 = jnp.bfloat16

SPANS = ((0, 384), (384, 384), (768, 256))
PARTS = range(3)
ROWS = 64
TILE = 256
LINE, PLANE, CUBE, FORWARD, SIBLING, COPIES = 0, 3, 6, 14, 18, 34
ITEMS = 16


def mod4(v):
    return lax.rem(v + 8, 4)


def position():
    rep = lax.axis_index("rep")
    fsdp = lax.axis_index("fsdp")
    x = lax.div(fsdp, 4) * 2 + lax.div(rep, 8)
    y = lax.rem(lax.div(rep, 2), 4)
    z = lax.rem(fsdp, 4)
    return x, y, z, lax.rem(rep, 2)


def device(x, y, z, core):
    return (lax.rem(x, 2) * 8 + y * 2 + core, lax.div(x, 2) * 4 + z)


def roles(part):
    return part % 3, (part + 1) % 3, (part + 2) % 3


def item_place(m):
    group = lax.div(m, 4)
    first, last = lax.div(3 - group, 3), lax.div(group, 3)
    middle = 1 - first - last
    shift = middle * (2 * lax.rem(m, 2) - 1) + 2 * last
    return shift, (first + last) * lax.rem(m, 4) + middle * (lax.div(m, 2) - 2)


def kernel(tokens, gain, deltas, steps, bucket, master, momentum,
           keys, master_out, momentum_out,
           tok, layer0, layer1, layer2, acc0, acc1, acc2, own, sib, pairs, landed, mas, mom, gain_v, steps_v, bucket_v,
           wcol, inv, out, local, pair_s, pair_r, red_s, red_r, gat_s, gat_r):
    layer = (layer0, layer1, layer2)
    acc = (acc0, acc1, acc2)
    here = position()
    x, y, z, core = here
    chip = lax.rem(x, 2) * 4 + y
    sibling = device(x, y, z, 1 - core)

    def columns(part):
        return pl.ds(*SPANS[part])

    def local_copy(src, dst, i):
        return pltpu.make_async_copy(src, dst, local.at[i])

    steps_copy = local_copy(steps, steps_v, 0)
    bucket_copy = local_copy(bucket, bucket_v, 1)
    gain_copy = local_copy(
        gain.at[pl.ds(pl.multiple_of(lax.axis_index("fsdp") * 1024, 1024), 1024)], gain_v, 2)
    mas_copy = local_copy(master, mas, 3)
    mom_copy = local_copy(momentum, mom, 4)
    own_copies = [local_copy(deltas.at[:, core, :, columns(p)], own.at[:, :, columns(p)], 5 + p) for p in PARTS]
    tok_copies = [
        local_copy(tokens.at[pl.ds(i * TILE, TILE)], tok.at[pl.ds(i * TILE, TILE)], 8 + i) for i in range(4)]
    for copy in [steps_copy, bucket_copy] + own_copies + [gain_copy, mas_copy, mom_copy] + tok_copies:
        copy.start()

    barrier = pltpu.get_barrier_semaphore()
    peers = [sibling]
    for d in range(1, 8):
        k = lax.rem(chip + d, 8)
        peers.append(device(lax.div(x, 2) * 2 + lax.div(k, 4), lax.rem(k, 4), z, core))
    far = (1 - lax.div(x, 2)) * 2
    peers.append(device(far, y, z, core))
    peers.append(device(far + 1, y, z, core))
    for d in range(1, 4):
        peers.append(device(x, y, mod4(z + d), core))
    for peer in peers:
        pl.semaphore_signal(barrier, inc=1, device_id=peer, device_id_type=MESH)
    pl.semaphore_wait(barrier, len(peers))

    pair_copies = [
        pltpu.make_async_remote_copy(
            src_ref=deltas.at[:, 1 - core, :, columns(p)], dst_ref=sib.at[:, :, columns(p)],
            send_sem=pair_s.at[p], recv_sem=pair_r.at[p], device_id=sibling, device_id_type=MESH)
        for p in PARTS]
    for copy in pair_copies:
        copy.start()

    steps_copy.wait()
    bucket_copy.wait()
    counts = steps_v[...].astype(F32)
    share = counts / jnp.sum(counts, axis=0, keepdims=True)
    replica = lax.axis_index("rep")
    replica_ids = lax.broadcasted_iota(jnp.int32, (16, 16), 0)
    lane = lax.broadcasted_iota(jnp.int32, (ROWS, 128), 1)
    row = lax.broadcasted_iota(jnp.int32, (ROWS, 128), 0)
    mine = lane == row + core * ROWS
    buckets = bucket_v[...]
    for side, who in enumerate((replica, replica + 1 - 2 * core)):
        row_share = jnp.sum(jnp.where(replica_ids == who, share, 0.0), axis=0, keepdims=True)
        weight = jnp.zeros((8, 128), F32)
        for b in range(16):
            weight = weight + jnp.where(buckets == b, row_share[:, b:b + 1], 0.0)
        for k in range(8):
            column = jnp.sum(jnp.where(mine, weight[k:k + 1, :], 0.0), axis=1, keepdims=True)
            wcol[side, k] = jnp.broadcast_to(column, (ROWS, 128))

    def reduce_copy(part, d):
        k = lax.rem(chip + d, 8)
        return pltpu.make_async_remote_copy(
            src_ref=pairs.at[k, :, columns(part)], dst_ref=landed.at[d - 1, :, columns(part)],
            send_sem=red_s.at[part, d - 1], recv_sem=red_r.at[part, d - 1],
            device_id=device(lax.div(x, 2) * 2 + lax.div(k, 4), lax.rem(k, 4), z, core), device_id_type=MESH)

    for p in PARTS:
        own_copies[p].wait()
        pair_copies[p].wait_recv()

        @pl.loop(0, 8)
        def _(k):
            w0 = wcol[0, k][:, :1]
            w1 = wcol[1, k][:, :1]
            both = w0 * own[k, :, columns(p)].astype(F32) + w1 * sib[k, :, columns(p)].astype(F32)
            pairs[k, :, columns(p)] = both.astype(BF16)

        @pl.loop(1, 8)
        def _(d):
            reduce_copy(p, d).start()

    for ref in acc:
        ref[...] = jnp.zeros_like(ref)
    gain_copy.wait()
    gain_rows = gain_v[...].astype(F32).reshape(8, 128)
    gain_row = jnp.sum(
        jnp.where(lax.broadcasted_iota(jnp.int32, (8, 128), 0) == chip, gain_rows, 0.0), axis=0, keepdims=True)
    gain_col = jnp.sum(jnp.where(mine, gain_row, 0.0), axis=1, keepdims=True)
    mas_copy.wait()
    mom_copy.wait()
    for copy in tok_copies:
        copy.wait()

    @pl.loop(0, 1024 // 32)
    def _(i):
        rows = pl.ds(pl.multiple_of(i * 32, 32), 32)
        total = jnp.zeros((32, 128), F32)
        for j in range(64):
            v = tok[rows, j * 128:(j + 1) * 128].astype(F32)
            total = total + v * v
        mean = jnp.sum(total, axis=1, keepdims=True) * (1.0 / 8192.0)
        inv[rows, :] = jnp.broadcast_to(lax.rsqrt(mean + EPSILON), (32, 128))

    def place(part):
        return [here[q] for q in roles(part)]

    def along(axis, d):
        moved = [mod4(v + d) if q == axis else v for q, v in enumerate((x, y, z))]
        return device(*moved, core)

    def gather_copy(part, ref, index, target):
        return pltpu.make_async_remote_copy(
            src_ref=ref, dst_ref=ref, send_sem=gat_s.at[part, index], recv_sem=gat_r.at[part, index],
            device_id=target, device_id_type=MESH)

    def line_send(part, d):
        i1, i2, i3 = place(part)
        return gather_copy(part, layer[part].at[i3, i2, i1, core], LINE + d - 1, along(roles(part)[0], d))

    def line_recv(part, d):
        i1, i2, i3 = place(part)
        return gather_copy(part, layer[part].at[i3, i2, mod4(i1 - d), core], LINE + d - 1, sibling)

    def a_line(part, m, who):
        shift, j = item_place(m)
        i1, i2, i3 = place(part)
        return layer[part].at[mod4(i3 + shift), mod4(i2 - j), :, who]

    def plane_send(part, d):
        return gather_copy(part, a_line(part, 0, core), PLANE + d - 1, along(roles(part)[1], d))

    def plane_recv(part, d):
        return gather_copy(part, a_line(part, d, core), PLANE + d - 1, sibling)

    def cube_send(part, way, j):
        return gather_copy(part, a_line(part, j, core), CUBE + 2 * j + way, along(roles(part)[2], 1 - 2 * way))

    def cube_recv(part, m):
        return gather_copy(part, a_line(part, m, core), CUBE + m - 4, sibling)

    def forward_send(part, m):
        way = lax.rem(m, 2)
        return gather_copy(
            part, a_line(part, m, core), FORWARD + lax.div(m, 2) - 2, along(roles(part)[2], 1 - 2 * way))

    def forward_recv(part, m):
        return gather_copy(part, a_line(part, m, core), FORWARD + m - 12, sibling)

    def sibling_send(part, m):
        return gather_copy(part, a_line(part, m, core), SIBLING + m, sibling)

    def sibling_recv(part, m):
        return gather_copy(part, a_line(part, m, 1 - core), SIBLING + m, sibling)

    def multiply(part, m):
        q1, q2, q3 = roles(part)
        i1, i2, i3 = place(part)
        shift, j = item_place(m)
        spot = [None, None, None]
        spot[q2] = mod4(i2 - j)
        spot[q3] = mod4(i3 + shift)
        weights = layer[part][spot[q3], spot[q2]].reshape(8 * ROWS, SPANS[part][1])
        left = []
        for i in range(4):
            spot[q1] = i
            start = lax.div(spot[0], 2) * 4096 + spot[2] * 1024 + lax.rem(spot[0], 2) * 512 + spot[1] * 128
            left.append(tok[:, pl.ds(pl.multiple_of(start, 128), 128)])
        acc[part][...] += jnp.dot(jnp.concatenate(left, axis=1), weights, preferred_element_type=F32)

    for p in PARTS:
        @pl.loop(1, 8)
        def _(d):
            reduce_copy(p, d).wait_recv()

        averaged = pairs[chip, :, columns(p)].astype(F32)
        for d in range(7):
            averaged = averaged + landed[d, :, columns(p)].astype(F32)
        momentum_new = MOMENTUM_KEEP * mom[:, columns(p)] + averaged
        master_new = mas[:, columns(p)] - OUTER_RATE * (averaged + MOMENTUM_KEEP * momentum_new)
        mom[:, columns(p)] = momentum_new
        mas[:, columns(p)] = master_new
        i1, i2, i3 = place(p)
        layer[p][i3, i2, i1, core] = (gain_col * master_new).astype(BF16)
        for d in (1, 3, 2):
            line_send(p, d).start()

    mas_back = local_copy(mas, master_out, 3)
    mom_back = local_copy(mom, momentum_out, 4)
    mas_back.start()
    mom_back.start()

    @pl.loop(0, ITEMS + 1)
    def _(m):
        for p in PARTS:
            @pl.when(m == 0)
            def _():
                for d in (1, 3, 2):
                    line_recv(p, d).wait_recv()
                for d in (1, 3, 2):
                    plane_send(p, d).start()

            @pl.when((m >= 1) & (m < 4))
            def _():
                plane_recv(p, m).wait_recv()

            @pl.when(m < 4)
            def _():
                cube_send(p, 0, m).start()
                cube_send(p, 1, m).start()

            @pl.when((m >= 4) & (m < 12))
            def _():
                cube_recv(p, m).wait_recv()

                @pl.when(lax.rem(lax.div(m, 2), 2) == lax.rem(m, 2))
                def _():
                    forward_send(p, m).start()

            @pl.when((m >= 12) & (m < ITEMS))
            def _():
                forward_recv(p, m).wait_recv()

            @pl.when(m < ITEMS)
            def _():
                sibling_send(p, m).start()

            @pl.when(m >= 1)
            def _():
                sibling_recv(p, m - 1).wait_recv()
                multiply(p, m - 1)

    def keys_copy(t):
        rows = pl.ds(pl.multiple_of(t * TILE, TILE), TILE)
        return pltpu.make_async_copy(out.at[rows], keys.at[rows], local.at[8 + t])

    @pl.loop(0, 1024 // TILE)
    def _(t):
        rows = pl.ds(pl.multiple_of(t * TILE, TILE), TILE)
        scale = inv[rows, :][:, :1]
        for p in PARTS:
            out[rows, columns(p)] = (acc[p][rows, :] * scale).astype(BF16)
        keys_copy(t).start()

    for p in PARTS:
        pair_copies[p].wait_send()

        @pl.loop(1, 8)
        def _(d):
            reduce_copy(p, d).wait_send()

        @pl.loop(1, 4)
        def _(d):
            line_send(p, d).wait_send()
            plane_send(p, d).wait_send()

        @pl.loop(0, 4)
        def _(j):
            cube_send(p, 0, j).wait_send()
            cube_send(p, 1, j).wait_send()
            forward_send(p, 2 * j + 4).wait_send()

        @pl.loop(0, ITEMS)
        def _(m):
            sibling_send(p, m).wait_send()

    mas_back.wait()
    mom_back.wait()

    @pl.loop(0, 1024 // TILE)
    def _(t):
        keys_copy(t).wait()


def on_device(tokens, norm_gain, deltas, inner_steps, bucket_of_row, master, momentum):
    hbm = pl.BlockSpec(memory_space=pl.ANY)
    dma = pltpu.SemaphoreType.DMA
    return pl.pallas_call(
        kernel,
        out_shape=(
            jax.ShapeDtypeStruct((1024, 1024), BF16),
            jax.ShapeDtypeStruct((ROWS, 1024), F32),
            jax.ShapeDtypeStruct((ROWS, 1024), F32),
        ),
        in_specs=[hbm] * 7,
        out_specs=(hbm, hbm, hbm),
        scratch_shapes=[
            pltpu.VMEM((1024, 8192), BF16),
            *[pltpu.VMEM((4, 4, 4, 2, ROWS, width), BF16) for _, width in SPANS],
            *[pltpu.VMEM((1024, width), F32) for _, width in SPANS],
            pltpu.VMEM((8, ROWS, 1024), BF16),
            pltpu.VMEM((8, ROWS, 1024), BF16),
            pltpu.VMEM((8, ROWS, 1024), BF16),
            pltpu.VMEM((7, ROWS, 1024), BF16),
            pltpu.VMEM((ROWS, 1024), F32),
            pltpu.VMEM((ROWS, 1024), F32),
            pltpu.VMEM((1024,), BF16),
            pltpu.VMEM((16, 16), jnp.int32),
            pltpu.VMEM((8, 128), jnp.int32),
            pltpu.VMEM((2, 8, ROWS, 128), F32),
            pltpu.VMEM((1024, 128), F32),
            pltpu.VMEM((1024, 1024), BF16),
            dma((12,)),
            dma((3,)),
            dma((3,)),
            dma((3, 7)),
            dma((3, 7)),
            dma((3, COPIES)),
            dma((3, COPIES)),
        ],
        compiler_params=pltpu.CompilerParams(
            collective_id=0, has_side_effects=True, vmem_limit_bytes=56 * 1024 * 1024),
        cost_estimate=pl.CostEstimate(flops=2 * 1024 * 8192 * 1024, bytes_accessed=24 << 20, transcendentals=1024),
    )(
        tokens,
        norm_gain,
        deltas.reshape(8, 2, ROWS, 1024),
        inner_steps,
        bucket_of_row.reshape(8, 128),
        master,
        momentum,
    )


def solution(mesh):
    in_specs = (
        P(("rep", "fsdp"), None),
        P(),
        P("rep", "fsdp", None),
        P(),
        P("fsdp"),
        P(("fsdp", "rep"), None),
        P(("fsdp", "rep"), None),
    )
    out_specs = (P(("rep", "fsdp"), None), P(("fsdp", "rep"), None), P(("fsdp", "rep"), None))
    return jax.shard_map(
        on_device, mesh=mesh, in_specs=in_specs, out_specs=out_specs, check_vma=False
    )
```

time: 118 us -> 86.1 us (0.73); the launches traced: 116 us -> 85.9 us
  Pallas kernels: 110 us -> 80.7 us
  other arithmetic: 1.34 us -> 0 us
    pallas_call x1, Pallas kernels: 110 us -> 80.7 us  [on_device(): pl.pallas_call(kernel, out_shape=(jax.ShapeDtypeStruct((1024, 1024), BF16...]
    reshape x1 -> x0, other arithmetic: 1.34 us -> none  [on_device(): norm_gain.astype(F32).reshape(64, 128)]
where the time goes in v2:
time: 86.1 us; the launch traced here: 85.9 us
  Pallas kernels  80.7 us (94%)
  local copies, waits for them, and re-layouts  4.55 us (5%)
    pallas_call x1, Pallas kernels, on_device(): pl.pallas_call(kernel, out_shape=(jax.ShapeDtypeStruct((1024, 1024), BF16...  80.7 us
    unnamed x7, local copies, waits for them, and re-layouts  4.55 us

profile of v2, /device:TPU:1, one launch (start us, length us, event | category | flops | bytes accessed | tf_op | source)
XLA Modules:
  0.0 85.9 jit_solution(12771993576567732064)
XLA Ops:
  0.6 80.7 %shard_map.94 = (bf16[1024,1024]{1,0:T(8,128)(2,1)}, f32[64,1024]{1,0:T(8,128)}, f32[64,1024]{1,0:T(8,128)}) custom-call(bf16[1024,8192]{1,0:T(8,128)(2,1)} %tokens.1, bf16[8192]{0:T(1024)(128)(2,1)} %gain.1, bf16[8,2,64,1024]{3,2,1,0:T(8,128)(2,1)} %bitcast.2, s32[16,16]{1,0:T(8,128)} %steps.1, s32[8,128]{1,0:T(8,128)} %bitcast.3, f32[64,1024]{1,0:T(8,128)} %master.1, ...), custom_call_target="tpu_custom_call" | custom-call | flops 17179869184 | bytes 25165824 | tf_op jit(solution)/shard_map/pallas_call | solution.py:339
  81.4 0.0 copy-start.1
  81.4 0.0 copy-start
  81.4 3.1 %copy.13 = bf16[1024,1024]{1,0:T(8,128)(2,1)} copy(bf16[1024,1024]{1,0:T(8,128)(2,1)} %get-tuple-element.6) | data formatting | bytes 4194304
  84.5 0.0 copy-done.1
  84.5 0.7 copy.14
  85.2 0.0 copy-done
  85.2 0.7 copy.15
Async XLA Ops:
  81.4 3.2 %copy-start.1 = (f32[64,1024]{1,0:T(8,128)S(1)}, f32[64,1024]{1,0:T(8,128)}, u32[]{:S(2)}) copy-start(f32[64,1024]{1,0:T(8,128)} %get-tuple-element.7) | copy-start | bytes 786436
  81.4 3.9 %copy-start = (f32[64,1024]{1,0:T(8,128)S(1)}, f32[64,1024]{1,0:T(8,128)}, u32[]{:S(2)}) copy-start(f32[64,1024]{1,0:T(8,128)} %get-tuple-element.8) | copy-start | bytes 786436

commit v3 on v2

--- a/solution.py
+++ b/solution.py
@@ -13,6 +13,7 @@
 BF16 = jnp.bfloat16
 
 SPANS = ((0, 384), (384, 384), (768, 256))
+ORDERS = ((1, 0, 2), (2, 1, 0), (0, 2, 1))
 PARTS = range(3)
 ROWS = 64
 TILE = 256
@@ -38,7 +39,7 @@
 
 
 def roles(part):
-    return part % 3, (part + 1) % 3, (part + 2) % 3
+    return ORDERS[part]
 
 
 def item_place(m):
@@ -333,16 +334,32 @@
         keys_copy(t).wait()
 
 
+def relay(keys, master_new, momentum_new, keys_out, master_out, momentum_out, keys_v, mas_v, mom_v, into, done):
+    spans = [pl.ds(i * TILE, TILE) for i in range(4)]
+    hops = [(keys.at[s], keys_v.at[s], keys_out.at[s]) for s in spans]
+    hops += [(master_new, mas_v, master_out), (momentum_new, mom_v, momentum_out)]
+    reads = [pltpu.make_async_copy(a, b, into.at[i]) for i, (a, b, _) in enumerate(hops)]
+    writes = [pltpu.make_async_copy(b, c, done.at[i]) for i, (_, b, c) in enumerate(hops)]
+    for copy in reads:
+        copy.start()
+    for read, write in zip(reads, writes):
+        read.wait()
+        write.start()
+    for copy in writes:
+        copy.wait()
+
+
 def on_device(tokens, norm_gain, deltas, inner_steps, bucket_of_row, master, momentum):
     hbm = pl.BlockSpec(memory_space=pl.ANY)
     dma = pltpu.SemaphoreType.DMA
-    return pl.pallas_call(
+    shapes = (
+        jax.ShapeDtypeStruct((1024, 1024), BF16),
+        jax.ShapeDtypeStruct((ROWS, 1024), F32),
+        jax.ShapeDtypeStruct((ROWS, 1024), F32),
+    )
+    results = pl.pallas_call(
         kernel,
-        out_shape=(
-            jax.ShapeDtypeStruct((1024, 1024), BF16),
-            jax.ShapeDtypeStruct((ROWS, 1024), F32),
-            jax.ShapeDtypeStruct((ROWS, 1024), F32),
-        ),
+        out_shape=shapes,
         in_specs=[hbm] * 7,
         out_specs=(hbm, hbm, hbm),
         scratch_shapes=[
@@ -381,6 +398,14 @@
         master,
         momentum,
     )
+    return pl.pallas_call(
+        relay,
+        out_shape=shapes,
+        in_specs=[hbm] * 3,
+        out_specs=(hbm, hbm, hbm),
+        scratch_shapes=[pltpu.VMEM(s.shape, s.dtype) for s in shapes] + [dma((6,)), dma((6,))],
+        compiler_params=pltpu.CompilerParams(vmem_limit_bytes=56 * 1024 * 1024),
+    )(*results)
 
 
 def solution(mesh):

time: 86.1 us -> 79.7 us (0.926)
  local copies, waits for them, and re-layouts: 4.55 us -> 0 us
  Pallas kernels: 80.7 us -> 78.9 us
    unnamed x7 -> x0, local copies, waits for them, and re-layouts: 4.55 us -> none
    pallas_call x1 -> x2, Pallas kernels: 80.7 us -> 78.9 us  [the longest x1 76.3 us: on_device(): pl.pallas_call(kernel, out_shape=shapes, in_specs=[hbm] * 7, out_specs=(h...]
where the time goes in v3:
time: 79.7 us; the launch traced here: 79.6 us
  Pallas kernels  78.9 us (99%)
    pallas_call x1, Pallas kernels, on_device(): pl.pallas_call(kernel, out_shape=shapes, in_specs=[hbm] * 7, out_specs=(h...  76.3 us
    pallas_call x1, Pallas kernels, on_device(): pl.pallas_call(relay, out_shape=shapes, in_specs=[hbm] * 3, out_specs=(hb...  2.63 us

profile of v3, /device:TPU:1, one launch (start us, length us, event | category | flops | bytes accessed | tf_op | source)
XLA Modules:
  0.0 79.6 jit_solution(15992100439598374909)
XLA Ops:
  0.6 76.3 %shard_map.94 = (bf16[1024,1024]{1,0:T(8,128)(2,1)}, f32[64,1024]{1,0:T(8,128)}, f32[64,1024]{1,0:T(8,128)}) custom-call(bf16[1024,8192]{1,0:T(8,128)(2,1)} %tokens.1, bf16[8192]{0:T(1024)(128)(2,1)} %gain.1, bf16[8,2,64,1024]{3,2,1,0:T(8,128)(2,1)} %bitcast.2, s32[16,16]{1,0:T(8,128)} %steps.1, s32[8,128]{1,0:T(8,128)} %bitcast.3, f32[64,1024]{1,0:T(8,128)} %master.1, ...), custom_call_target="tpu_custom_call" | custom-call | flops 17179869184 | bytes 25165824 | tf_op jit(solution)/shard_map/pallas_call | solution.py:360
  76.9 2.6 %shard_map.95 = (bf16[1024,1024]{1,0:T(8,128)(2,1)}, f32[64,1024]{1,0:T(8,128)}, f32[64,1024]{1,0:T(8,128)}) custom-call(bf16[1024,1024]{1,0:T(8,128)(2,1)} %get-tuple-element.6.keys, f32[64,1024]{1,0:T(8,128)} %get-tuple-element.7.master_new, f32[64,1024]{1,0:T(8,128)} %get-tuple-element.8.momentum_new), custom_call_target="tpu_custom_call" | custom-call | tf_op jit(solution)/shard_map/pallas_call | solution.py:401

commit v4 on v3

--- a/solution.py
+++ b/solution.py
@@ -334,18 +334,15 @@
         keys_copy(t).wait()
 
 
-def relay(keys, master_new, momentum_new, keys_out, master_out, momentum_out, keys_v, mas_v, mom_v, into, done):
-    spans = [pl.ds(i * TILE, TILE) for i in range(4)]
-    hops = [(keys.at[s], keys_v.at[s], keys_out.at[s]) for s in spans]
-    hops += [(master_new, mas_v, master_out), (momentum_new, mom_v, momentum_out)]
-    reads = [pltpu.make_async_copy(a, b, into.at[i]) for i, (a, b, _) in enumerate(hops)]
-    writes = [pltpu.make_async_copy(b, c, done.at[i]) for i, (_, b, c) in enumerate(hops)]
-    for copy in reads:
+def relay(keys, master_new, momentum_new, keys_out, master_out, momentum_out, done):
+    copies = [
+        pltpu.make_async_copy(keys.at[pl.ds(i * TILE, TILE)], keys_out.at[pl.ds(i * TILE, TILE)], done.at[i])
+        for i in range(4)]
+    copies.append(pltpu.make_async_copy(master_new, master_out, done.at[4]))
+    copies.append(pltpu.make_async_copy(momentum_new, momentum_out, done.at[5]))
+    for copy in copies:
         copy.start()
-    for read, write in zip(reads, writes):
-        read.wait()
-        write.start()
-    for copy in writes:
+    for copy in copies:
         copy.wait()
 
 
@@ -387,24 +384,25 @@
             dma((3, COPIES)),
         ],
         compiler_params=pltpu.CompilerParams(
-            collective_id=0, has_side_effects=True, vmem_limit_bytes=56 * 1024 * 1024),
+            collective_id=0, has_side_effects=True, vmem_limit_bytes=50 * 1024 * 1024),
         cost_estimate=pl.CostEstimate(flops=2 * 1024 * 8192 * 1024, bytes_accessed=24 << 20, transcendentals=1024),
     )(
+        *[pltpu.with_memory_space_constraint(v, pltpu.HBM) for v in (
         tokens,
         norm_gain,
         deltas.reshape(8, 2, ROWS, 1024),
         inner_steps,
         bucket_of_row.reshape(8, 128),
         master,
-        momentum,
+        momentum)],
     )
     return pl.pallas_call(
         relay,
         out_shape=shapes,
-        in_specs=[hbm] * 3,
+        in_specs=[pl.BlockSpec(memory_space=pltpu.VMEM)] * 3,
         out_specs=(hbm, hbm, hbm),
-        scratch_shapes=[pltpu.VMEM(s.shape, s.dtype) for s in shapes] + [dma((6,)), dma((6,))],
-        compiler_params=pltpu.CompilerParams(vmem_limit_bytes=56 * 1024 * 1024),
+        scratch_shapes=[dma((6,))],
+        compiler_params=pltpu.CompilerParams(vmem_limit_bytes=16 * 1024 * 1024),
     )(*results)
 
 

time: 79.7 us -> 78.5 us (0.985)
  Pallas kernels: 78.9 us -> 77.8 us
    pallas_call x1, Pallas kernels: 2.63 us -> 1.53 us  [on_device(): pl.pallas_call(relay, out_shape=shapes, in_specs=[pl.BlockSpec(memory_spa...]
where the time goes in v4:
time: 78.5 us; the launch traced here: 78.4 us
  Pallas kernels  77.8 us (99%)
    pallas_call x1, Pallas kernels, on_device(): pl.pallas_call(kernel, out_shape=shapes, in_specs=[hbm] * 7, out_specs=(h...  76.2 us

profile of v4, /device:TPU:1, one launch (start us, length us, event | category | flops | bytes accessed | tf_op | source)
XLA Modules:
  0.0 78.4 jit_solution(8619899030285152680)
XLA Ops:
  0.6 76.2 %shard_map.94 = (bf16[1024,1024]{1,0:T(8,128)(2,1)S(1)}, f32[64,1024]{1,0:T(8,128)S(1)}, f32[64,1024]{1,0:T(8,128)S(1)}) custom-call(bf16[1024,8192]{1,0:T(8,128)(2,1)} %tokens.1, bf16[8192]{0:T(1024)(128)(2,1)} %gain.1, bf16[8,2,64,1024]{3,2,1,0:T(8,128)(2,1)} %bitcast.2, s32[16,16]{1,0:T(8,128)} %steps.1, s32[8,128]{1,0:T(8,128)} %bitcast.3, ...), custom_call_target="tpu_custom_call" | custom-call | flops 17179869184 | bytes 25165824 | tf_op jit(solution)/shard_map/pallas_call | solution.py:357
  76.9 1.5 %shard_map.95 = (bf16[1024,1024]{1,0:T(8,128)(2,1)}, f32[64,1024]{1,0:T(8,128)}, f32[64,1024]{1,0:T(8,128)}) custom-call(bf16[1024,1024]{1,0:T(8,128)(2,1)S(1)} %get-tuple-element.6.keys, f32[64,1024]{1,0:T(8,128)S(1)} %get-tuple-element.7.master_new, f32[64,1024]{1,0:T(8,128)S(1)} %get-tuple-element.8.momentum_new), custom_call_target="tpu_custom_call" | custom-call | tf_op jit(solution)/shard_map/pallas_call | solution.py:399

commit v5 on v4

--- a/solution.py
+++ b/solution.py
@@ -254,7 +254,7 @@
 
     @pl.loop(0, ITEMS + 1)
     def _(m):
-        for p in PARTS:
+        for p in (2, 0, 1):
             @pl.when(m == 0)
             def _():
                 for d in (1, 3, 2):

time: 78.5 us -> 82.9 us (1.056)
  Pallas kernels: 77.8 us -> 82.2 us
    pallas_call x1, Pallas kernels: 76.2 us -> 80.6 us  [on_device(): pl.pallas_call(kernel, out_shape=shapes, in_specs=[hbm] * 7, out_specs=(h...]
where the time goes in v5:
time: 82.9 us; the launch traced here: 82.8 us
  Pallas kernels  82.2 us (99%)
    pallas_call x1, Pallas kernels, on_device(): pl.pallas_call(kernel, out_shape=shapes, in_specs=[hbm] * 7, out_specs=(h...  80.6 us

profile of v5, /device:TPU:1, one launch (start us, length us, event | category | flops | bytes accessed | tf_op | source)
XLA Modules:
  0.0 82.8 jit_solution(9395192977337753006)
XLA Ops:
  0.6 80.6 %shard_map.94 = (bf16[1024,1024]{1,0:T(8,128)(2,1)S(1)}, f32[64,1024]{1,0:T(8,128)S(1)}, f32[64,1024]{1,0:T(8,128)S(1)}) custom-call(bf16[1024,8192]{1,0:T(8,128)(2,1)} %tokens.1, bf16[8192]{0:T(1024)(128)(2,1)} %gain.1, bf16[8,2,64,1024]{3,2,1,0:T(8,128)(2,1)} %bitcast.2, s32[16,16]{1,0:T(8,128)} %steps.1, s32[8,128]{1,0:T(8,128)} %bitcast.3, ...), custom_call_target="tpu_custom_call" | custom-call | flops 17179869184 | bytes 25165824 | tf_op jit(solution)/shard_map/pallas_call | solution.py:357
  81.3 1.5 %shard_map.95 = (bf16[1024,1024]{1,0:T(8,128)(2,1)}, f32[64,1024]{1,0:T(8,128)}, f32[64,1024]{1,0:T(8,128)}) custom-call(bf16[1024,1024]{1,0:T(8,128)(2,1)S(1)} %get-tuple-element.6.keys, f32[64,1024]{1,0:T(8,128)S(1)} %get-tuple-element.7.master_new, f32[64,1024]{1,0:T(8,128)S(1)} %get-tuple-element.8.momentum_new), custom_call_target="tpu_custom_call" | custom-call | tf_op jit(solution)/shard_map/pallas_call | solution.py:399
